TPU v7x, 512 devices: a whole 4x4x16 slice. The times are simulated.
512 devices in a mesh: ctx: 32 (over z, core), ch: 16 (over x, y).
Axes of the slice: x: 4, y: 4, z: 16, core: 2. Of those that a mesh axis runs over, the one named last changes fastest.
Arguments:
- query_in: bfloat16 [8192, 4096], P('ctx', 'ch'), may hold values from -63 to 63
- key_in: bfloat16 [8192, 4096], P('ctx', 'ch'), may hold values from -4 to 4
- value_in: bfloat16 [8192, 4096], P('ctx', 'ch'), may hold values from -4 to 4
- short_taps: float32 [7, 3, 4096], P(None, None, 'ch'), may hold values from -2 to 2
- residues: float32 [4096, 16], P('ch'), may hold values from -1.5 to 1.5
- decays: float32 [4096, 16], P('ch'), may hold values from 6.1035157e-06 to 0.02
- out_weight: bfloat16 [4096, 4096], P('ch'), may hold values from -0.125 to 0.125
- out_grad: bfloat16 [8192, 4096], P('ctx', 'ch'), may hold values from -6 to 6
Outputs:
- projected: bfloat16 [8192, 4096], P('ctx', 'ch')
- grad_query: bfloat16 [8192, 4096], P('ctx', 'ch')
- grad_key: bfloat16 [8192, 4096], P('ctx', 'ch')
- grad_value: bfloat16 [8192, 4096], P('ctx', 'ch')
All inputs are finite; a program needn't handle non-finite values.
Results may differ from a plain program's by a relative error of at most 0.0058.
Values may be sent and summed in bfloat16 or wider, within the bound.
A program may use at most 64 MiB of HBM per device.

v0:
```python
import jax
import jax.numpy as jnp
import numpy as np
from jax import lax
from jax.sharding import PartitionSpec as P

block_len = 64
exact_precision = lax.Precision.HIGHEST


def from_behind(value, axis, steps):
    count = lax.axis_size(axis)
    leading, last = (max(0, -steps), min(count, count - steps))
    return lax.ppermute(value, axis, [(source, source + steps) for source in range(leading, last)])


def one_hot_table():
    indices = np.arange(block_len)
    return (indices[None, :, None] - indices[None, None, :] == indices[:, None, None]).astype(
        np.float32
    )


def modal_tables(residues, decays):
    offsets = jnp.arange(block_len, dtype=jnp.float32)
    scaled = residues * jnp.sqrt(decays)
    filter_head = jnp.einsum(
        "cn,cnd->cd", scaled, jnp.exp(-decays[:, :, None] * offsets), precision=exact_precision
    )
    toeplitz = jnp.einsum(
        "cd,dij->cij", filter_head, jnp.asarray(one_hot_table()), precision=exact_precision
    )
    decay_in = jnp.exp(-decays[:, :, None] * (block_len - 1.0 - offsets))
    decay_out = scaled[:, :, None] * jnp.exp(-decays[:, :, None] * (offsets + 1.0))
    return (toeplitz, decay_in, decay_out)


def combine(earlier, latter):
    return (earlier[0] * latter[1] + latter[0], earlier[1] * latter[1])


def prepare(signal, decays, decay_tables):
    channels, length = signal.shape
    pieces = length // block_len
    block_list = signal.reshape(channels, pieces, block_len)
    within_block = jnp.einsum(
        "cij,cbj->cbi", decay_tables[0], block_list, precision=exact_precision
    )
    block_final_states = jnp.einsum(
        "avp,axp->avx", block_list, decay_tables[1], precision=exact_precision
    )
    factor = jnp.broadcast_to(jnp.exp(-decays * block_len)[:, None, :], block_final_states.shape)
    running, _ = lax.associative_scan(combine, (block_final_states, factor), axis=1)
    return (within_block, running)


def finish(within_block, running, decays, incoming, decay_tables):
    channels, pieces, _ = within_block.shape
    earlier_sum = jnp.concatenate([jnp.zeros_like(running[:, :1]), running[:, :-1]], axis=1)
    starts = jnp.arange(pieces, dtype=jnp.float32) * block_len
    carried_state = (
        earlier_sum + jnp.exp(-decays[:, None, :] * starts[None, :, None]) * incoming[:, None, :]
    )
    final_output = within_block + jnp.einsum(
        "lpe,leo->lpo", carried_state, decay_tables[2], precision=exact_precision
    )
    return final_output.reshape(channels, pieces * block_len)


def channel_params(residues, decays):
    part_size = residues.shape[0] // lax.axis_size("ctx")
    first_chan = lax.axis_index("ctx") * part_size
    residues = lax.dynamic_slice_in_dim(residues, first_chan, part_size, 0)
    decays = lax.dynamic_slice_in_dim(decays, first_chan, part_size, 0)
    return (decays, modal_tables(residues, decays))


def long_forward(mixed_values, decays, decay_tables):
    sequence = lax.all_to_all(mixed_values.T, "ctx", split_axis=0, concat_axis=1, tiled=True)
    within_block, running = prepare(sequence.astype(jnp.float32), decays, decay_tables)
    final_output = finish(
        within_block, running, decays, jnp.zeros(decays.shape, jnp.float32), decay_tables
    )
    return lax.all_to_all(final_output, "ctx", split_axis=1, concat_axis=0, tiled=True).T


def long_backward(grad_mixed, decays, decay_tables):
    sequence = lax.all_to_all(grad_mixed.T, "ctx", split_axis=0, concat_axis=1, tiled=True)
    within_block, running = prepare(jnp.flip(sequence.astype(jnp.float32), 1), decays, decay_tables)
    final_output = jnp.flip(
        finish(within_block, running, decays, jnp.zeros(decays.shape, jnp.float32), decay_tables), 1
    )
    return lax.all_to_all(final_output, "ctx", split_axis=1, concat_axis=0, tiled=True).T


def shards(query_in, key_in, value_in, short_taps, residues, decays, out_weight, out_grad):
    length = query_in.shape[0]
    rim_len = short_taps.shape[0] - 1
    stacked = jnp.stack([query_in, key_in, value_in])
    ahead_rows = from_behind(stacked[:, length - rim_len :], "ctx", 1)
    extended = jnp.concatenate([ahead_rows, stacked], axis=1).astype(jnp.float32)
    featured = jnp.zeros(stacked.shape, jnp.float32)
    for tap_index in range(rim_len + 1):
        begin = rim_len - tap_index
        featured = (
            featured + short_taps[tap_index][:, None, :] * extended[:, begin : begin + length]
        )
    query_feat = featured[0]
    key_feat = featured[1]
    value_feat = featured[2]
    mixed_values = (key_feat * value_feat).astype(jnp.bfloat16)
    used_decays, decay_tables = channel_params(residues, decays)
    conv_out = long_forward(mixed_values, used_decays, decay_tables)
    gated = (query_feat * conv_out).astype(jnp.bfloat16)
    partial_proj = jnp.dot(gated, out_weight, preferred_element_type=jnp.float32)
    projected = lax.psum_scatter(partial_proj, "ch", scatter_dimension=1, tiled=True).astype(
        jnp.bfloat16
    )
    grad_gated = jnp.einsum(
        "te,ce->tc",
        lax.all_gather(out_grad, "ch", axis=1, tiled=True),
        out_weight,
        preferred_element_type=jnp.float32,
    )
    grad_query_feat = (grad_gated * conv_out).astype(jnp.bfloat16)
    grad_mixed = (grad_gated * query_feat).astype(jnp.bfloat16)
    grad_conv = long_backward(grad_mixed, used_decays, decay_tables)
    grad_key_feat = (grad_conv * value_feat).astype(jnp.bfloat16)
    grad_value_feat = (grad_conv * key_feat).astype(jnp.bfloat16)
    grad_feats = jnp.stack([grad_query_feat, grad_key_feat, grad_value_feat])
    behind = from_behind(grad_feats[:, :rim_len], "ctx", -1)
    widened = jnp.concatenate([grad_feats, behind], axis=1).astype(jnp.float32)
    grad_stack = jnp.zeros(grad_feats.shape, jnp.float32)
    for tap_index in range(rim_len + 1):
        grad_stack = (
            grad_stack
            + short_taps[tap_index][:, None, :] * widened[:, tap_index : tap_index + length]
        )
    grad_stack = grad_stack.astype(jnp.bfloat16)
    return (projected, grad_stack[0], grad_stack[1], grad_stack[2])


def solution(mesh):
    in_specs = (
        P("ctx", "ch"),
        P("ctx", "ch"),
        P("ctx", "ch"),
        P(None, None, "ch"),
        P("ch", None),
        P("ch", None),
        P("ch", None),
        P("ctx", "ch"),
    )
    out_specs = (P("ctx", "ch"), P("ctx", "ch"), P("ctx", "ch"), P("ctx", "ch"))
    return jax.shard_map(shards, mesh=mesh, in_specs=in_specs, out_specs=out_specs, check_vma=False)
```

profile of v0, /device:TPU:32, one launch (start us, length us, event | category | flops | bytes accessed | tf_op | source)
XLA Modules:
  0.0 459.0 jit_solution(5360661742519281431)
XLA Ops:
  8.6 1.9 collective-permute-start
  18.3 59.2 %all-gather.2.cloned.1.call-done = bf16[256,4096]{1,0:T(8,128)(2,1)} async-done(((bf16[256,256]{1,0:T(8,128)(2,1)}), bf16[256,4096]{1,0:T(8,128)(2,1)}) %all-gather.2.cloned.1.call-update) | async-done | bytes 2097168 | tf_op jit(solution)/shard_map/all_gather | solution.py:121
  77.4 2.3 fusion.74
  80.6 12.8 %all-to-all-start.2 = ((bf16[32,8,256]{2,1,0:T(8,128)(2,1)}), bf16[32,8,256]{2,1,0:T(8,128)(2,1)S(1)}, u32[]{:S(2)}, u32[]{:S(2)}) async-start(bf16[32,8,256]{2,1,0:T(8,128)(2,1)} %bitcast.21), calls=%async_computation.3 | async-start | bytes 262144 | tf_op jit(solution)/shard_map/all_to_all | solution.py:88
  93.9 3.4 fusion.73
  97.3 11.8 %all-to-all-done.2 = bf16[32,8,256]{2,1,0:T(8,128)(2,1)S(1)} async-done(((bf16[32,8,256]{2,1,0:T(8,128)(2,1)}), bf16[32,8,256]{2,1,0:T(8,128)(2,1)S(1)}, u32[]{:S(2)}, u32[]{:S(2)}) %all-to-all-start.2) | async-done | bytes 131104 | tf_op jit(solution)/shard_map/all_to_all | solution.py:88
  109.1 21.2 %rev.7 = f32[8,8192]{1,0:T(8,128)} reverse(f32[8,8192]{1,0:T(8,128)S(1)} %bitcast.137), dimensions={1} | reverse | bytes 524288 | tf_op jit(solution)/shard_map/jit(_flip)/rev | solution.py:89
  131.5 1.6 fusion.42
  133.0 1.8 slice.453
  136.0 1.8 slice.423
  146.2 1.6 multiply_add_fusion.3
  147.7 1.6 slice.447
  149.4 1.7 slice.433
  151.1 1.7 slice.432
  152.7 1.6 multiply_add_fusion.2
  154.3 1.6 slice.445
  155.9 1.6 slice.436
  157.5 1.6 slice.435
  161.4 2.8 fusion.17
  170.7 3.2 pad.107
  176.2 3.2 pad.109
  186.3 1.6 pad.161
  187.9 1.6 pad.217
  189.5 2.1 convolution_add_fusion
  193.7 24.0 %rev.8 = f32[8,8192]{1,0:T(8,128)S(1)} reverse(f32[8,8192]{1,0:T(8,128)} %reshape.69), dimensions={1} | reverse | bytes 524288 | tf_op jit(solution)/shard_map/jit(_flip)/rev | solution.py:90
  217.7 26.1 %all_to_all.67 = f32[8,32,256]{2,0,1:T(8,128)} all-to-all(f32[8,32,256]{2,0,1:T(8,128)S(1)} %bitcast.138), channel_id=1, replica_groups=mesh['ctx'=32,'ch'=16] {'ctx'}, dimensions={1} | all-to-all | bytes 524288 | tf_op jit(solution)/shard_map/all_to_all | solution.py:93
  246.7 20.7 %all_to_all.68 = bf16[32,8,256]{2,1,0:T(8,128)(2,1)S(1)} all-to-all(bf16[32,8,256]{2,1,0:T(8,128)(2,1)S(1)} %bitcast.147), channel_id=1, replica_groups=mesh['ctx'=32,'ch'=16] {'ctx'}, dimensions={0} | all-to-all | bytes 262144 | tf_op jit(solution)/shard_map/all_to_all | solution.py:79
  269.1 1.3 fusion.19
  271.6 1.8 slice.420
  285.0 1.6 fusion.71
  287.3 3.1 pad.91
  294.3 4.9 %pad.92 = f32[8,8,16]{1,2,0:T(8,128)} pad(f32[8,4,16]{1,2,0:T(8,128)} %pad_maximum_fusion.1, f32[]{:T(128)} %constant.7.clone.1), padding=0_0_0x0_1_1x0_0_0 | pad | bytes 6148 | tf_op jit(solution)/shard_map/pad | solution.py:53
  299.2 4.9 %pad.93 = f32[8,8,16]{1,2,0:T(8,128)} pad(f32[8,4,16]{1,2,0:T(8,128)} %add.260, f32[]{:T(128)} %constant.7.clone.1), padding=0_0_0x1_0_1x0_0_0 | pad | bytes 6148 | tf_op jit(solution)/shard_map/pad | solution.py:53
  304.1 1.5 add.262
  307.3 3.2 pad.94
  310.5 5.0 %pad.95 = f32[8,16,16]{1,2,0:T(8,128)} pad(f32[8,8,16]{1,2,0:T(8,128)} %add.262, f32[]{:T(128)} %constant.7.clone.1), padding=0_0_0x1_0_1x0_0_0 | pad | bytes 12292 | tf_op jit(solution)/shard_map/pad | solution.py:53
  315.5 1.5 add.264
  318.8 3.3 pad.97
  324.8 3.5 pad.99
  329.3 1.6 pad.159
  330.9 1.6 pad.216
  332.6 2.1 convolution_add_fusion.1
  337.8 25.2 %all_to_all.69 = f32[8,32,256]{2,0,1:T(8,128)S(1)} all-to-all(f32[8,32,256]{2,0,1:T(8,128)S(1)} %copy.85), channel_id=1, replica_groups=mesh['ctx'=32,'ch'=16] {'ctx'}, dimensions={1} | all-to-all | bytes 524288 | tf_op jit(solution)/shard_map/all_to_all | solution.py:84
  363.2 2.7 fusion.24
  366.9 2.5 collective-permute-start.1
  369.5 1.4 collective-permute-done.1
  372.4 78.1 %reduce-scatter.2.cloned.1.call-done = f32[256,256]{1,0:T(8,128)} async-done(((f32[256,4096]{1,0:T(8,128)}), f32[256,256]{1,0:T(8,128)}) %reduce-scatter.2.cloned.1.call-update) | async-done | bytes 262160 | tf_op jit(solution)/shard_map/reduce_scatter | solution.py:116
  450.5 1.6 convert_element_type.43
  (187 shorter events, 75.7 us)
Async XLA Ops:
  7.2 70.3 %copy-start = (bf16[256,4096]{1,0:T(8,128)(2,1)S(1)}, bf16[256,4096]{1,0:T(8,128)(2,1)}, u32[]{:S(2)}) copy-start(bf16[256,4096]{1,0:T(8,128)(2,1)} %param.15) | copy-start | bytes 6291460
  7.2 70.2 %all-gather.2.cloned.1.call-start = ((), (), s32[]{:S(2)}) async-start(), calls=%async_computation.6 | async-start | bytes 2228224 | tf_op jit(solution)/shard_map/all_gather | solution.py:121
  8.6 7.8 %collective-permute-start = (bf16[3,6,256]{2,1,0:T(8,128)(2,1)S(1)}, bf16[3,6,256]{2,1,0:T(8,128)(2,1)S(1)}, u32[]{:S(2)}, u32[]{:S(2)}) collective-permute-start(bf16[3,6,256]{2,1,0:T(8,128)(2,1)S(1)} %pad_maximum_fusion.14), channel_id=1, source_target_pairs={{0,16},{16,32},{32,48},{48,64},{64,80},{80,96},{96,112},{112,128},... | collective-permute-start | bytes 27656 | tf_op jit(solution)/shard_map/ppermute | solution.py:14
  13.6 4.6 copy-start.16
  13.6 4.6 copy-start.18
  13.7 4.5 copy-start.20
  13.7 4.5 copy-start.22
  13.7 4.5 copy-start.24
  13.7 4.5 copy-start.26
  14.3 79.3 %copy-start.14 = (f32[8,16]{1,0:T(8,128)}, f32[8,16]{1,0:T(8,128)S(1)}, u32[]{:S(2)}) copy-start(f32[8,16]{1,0:T(8,128)S(1)} %get-tuple-element.34) | copy-start | bytes 1540
  14.9 3.3 copy-start.28
  79.8 29.4 %copy-start.1 = (f32[256,256]{1,0:T(8,128)}, f32[256,256]{1,0:T(8,128)S(1)}, u32[]{:S(2)}) copy-start(f32[256,256]{1,0:T(8,128)S(1)} %fusion.74) | copy-start | bytes 786436
  80.6 28.5 %all-to-all-start.2 = ((bf16[32,8,256]{2,1,0:T(8,128)(2,1)}), bf16[32,8,256]{2,1,0:T(8,128)(2,1)S(1)}, u32[]{:S(2)}, u32[]{:S(2)}) async-start(bf16[32,8,256]{2,1,0:T(8,128)(2,1)} %bitcast.21), calls=%async_computation.3 | async-start | bytes 262144 | tf_op jit(solution)/shard_map/all_to_all | solution.py:88
  93.4 357.1 %reduce-scatter.2.cloned.1.call-start = ((), (), s32[]{:S(2)}) async-start(), calls=%async_computation.5 | async-start | bytes 4456448 | tf_op jit(solution)/shard_map/reduce_scatter | solution.py:116
  133.0 4.7 %copy-start.8 = (f32[8,128,16]{1,2,0:T(8,128)}, f32[8,128,16]{1,2,0:T(8,128)S(1)}, u32[]{:S(2)}) copy-start(f32[8,128,16]{1,2,0:T(8,128)S(1)} %fusion.42) | copy-start | bytes 196612
  143.3 15.8 %copy-start.4 = (f32[8,32,16]{1,2,0:T(8,128)}, f32[8,32,16]{1,2,0:T(8,128)S(1)}, u32[]{:S(2)}) copy-start(f32[8,32,16]{1,2,0:T(8,128)S(1)} %multiply_add_fusion.4) | copy-start | bytes 49156
  164.2 5.8 %copy-start.7 = (f32[8,8,16]{1,2,0:T(8,128)S(1)}, f32[8,8,16]{1,2,0:T(8,128)}, u32[]{:S(2)}) copy-start(f32[8,8,16]{1,2,0:T(8,128)} %multiply_add_fusion.2) | copy-start | bytes 12292
  164.2 11.2 %copy-start.6 = (f32[8,16,16]{1,2,0:T(8,128)S(1)}, f32[8,16,16]{1,2,0:T(8,128)}, u32[]{:S(2)}) copy-start(f32[8,16,16]{1,2,0:T(8,128)} %multiply_add_fusion.3) | copy-start | bytes 24580
  164.2 16.2 %copy-start.5 = (f32[8,32,16]{1,2,0:T(8,128)S(1)}, f32[8,32,16]{1,2,0:T(8,128)}, u32[]{:S(2)}) copy-start(f32[8,32,16]{1,2,0:T(8,128)} %copy-done.4) | copy-start | bytes 49156
  168.4 17.8 %copy-start.9 = (f32[8,128,16]{1,2,0:T(8,128)S(1)}, f32[8,128,16]{1,2,0:T(8,128)}, u32[]{:S(2)}) copy-start(f32[8,128,16]{1,2,0:T(8,128)} %copy-done.8) | copy-start | bytes 196612
  170.1 19.5 %copy-start.12 = (f32[8,128,64]{1,2,0:T(8,128)S(1)}, f32[8,128,64]{1,2,0:T(8,128)}, u32[]{:S(2)}) copy-start(f32[8,128,64]{1,2,0:T(8,128)} %fusion.17) | copy-start | bytes 786436
  193.7 75.4 %copy-start.3 = (f32[8,64,64]{2,0,1:T(8,128)S(1)}, f32[8,64,64]{2,0,1:T(8,128)}, u32[]{:S(2)}) copy-start(f32[8,64,64]{2,0,1:T(8,128)} %fusion.73) | copy-start | bytes 393220
  271.6 9.6 %copy-start.13 = (f32[8,16]{1,0:T(8,128)S(1)}, f32[8,16]{1,0:T(8,128)}, u32[]{:S(2)}) copy-start(f32[8,16]{1,0:T(8,128)} %get-tuple-element.30) | copy-start | bytes 1540
  294.3 38.3 %copy-start.11 = (f32[8,128,64]{1,2,0:T(8,128)S(1)}, f32[8,128,64]{1,2,0:T(8,128)}, u32[]{:S(2)}) copy-start(f32[8,128,64]{1,2,0:T(8,128)} %fusion.19) | copy-start | bytes 786436
  317.9 14.7 %copy-start.15 = (f32[8,16]{1,0:T(8,128)S(1)}, f32[8,16]{1,0:T(8,128)}, u32[]{:S(2)}) copy-start(f32[8,16]{1,0:T(8,128)} %copy-done.14) | copy-start | bytes 1540
  365.9 0.9 copy-start.2
  365.9 1.0 copy-start.10
  366.8 4.1 copy-start.17
  366.8 4.1 copy-start.19
  366.8 4.1 copy-start.21
  366.8 4.1 copy-start.23
  366.8 4.1 copy-start.25
  366.8 4.1 copy-start.27
  366.8 4.1 copy-start.29
  366.9 3.9 collective-permute-start.1
Sparse Core Ops, SparseCore 0:
  11.0 66.3 all-gather.1
  366.0 84.4 reduce-scatter.1
where the time goes:
time: 464 us; the launch traced here: 459 us
  waiting for transfers between devices  151 us (33%)
  local copies, waits for them, and re-layouts  144 us (31%)
  blocking collectives  72 us (16%)
  other arithmetic  40 us (9%)
  matrix products  19.7 us (4%)
  starting transfers between devices  17.5 us (4%)
  between operations  15 us (3%)
    reduce_scatter x1, waiting for transfers between devices, shards(): lax.psum_scatter(partial_proj, 'ch', scatter_dimension=1, tiled=True)  78.1 us
    all_gather x1, waiting for transfers between devices, shards(): lax.all_gather(out_grad, 'ch', axis=1, tiled=True)  59.2 us
    pad x20, local copies, waits for them, and re-layouts, prepare(): lax.associative_scan(combine, (block_final_states, factor), axis=1)  42.8 us
    slice x34, local copies, waits for them, and re-layouts, prepare(): lax.associative_scan(combine, (block_final_states, factor), axis=1)  32.8 us
    all_to_all x1, blocking collectives, long_backward(): lax.all_to_all(final_output, 'ctx', split_axis=1, concat_axis=0, tiled=True)  26.1 us
    all_to_all x1, blocking collectives, long_forward(): lax.all_to_all(final_output, 'ctx', split_axis=1, concat_axis=0, tiled=True)  25.2 us
    rev x1, local copies, waits for them, and re-layouts, long_backward(): jnp.flip(finish(within_block, running, decays, jnp.zeros(decays.shape, jn...  24 us
    rev x1, local copies, waits for them, and re-layouts, long_backward(): jnp.flip(sequence.astype(jnp.float32), 1)  21.2 us
  transfers between devices with their start and end apart: 5, of which 4 were waited for; matrix products, arithmetic and copies ran while one was open for 3% of the time, Pallas kernels for 0%

commit v1 on v0

--- a/solution.py
+++ b/solution.py
@@ -6,6 +6,11 @@
 
 block_len = 64
 exact_precision = lax.Precision.HIGHEST
+
+
+def swapped_in(x, name, along):
+    sent = jnp.stack([x] * lax.axis_size(name))
+    return jnp.concatenate(lax.all_to_all(sent, name, 0, 0), axis=along)
 
 
 def from_behind(value, axis, steps):
@@ -117,10 +122,7 @@
         jnp.bfloat16
     )
     grad_gated = jnp.einsum(
-        "te,ce->tc",
-        lax.all_gather(out_grad, "ch", axis=1, tiled=True),
-        out_weight,
-        preferred_element_type=jnp.float32,
+        "te,ce->tc", swapped_in(out_grad, "ch", 1), out_weight, preferred_element_type=jnp.float32
     )
     grad_query_feat = (grad_gated * conv_out).astype(jnp.bfloat16)
     grad_mixed = (grad_gated * query_feat).astype(jnp.bfloat16)

time: 464 us -> 442 us (0.953)
  waiting for transfers between devices: 151 us -> 119 us
  starting transfers between devices: 17.5 us -> 28.1 us
    all_gather x1 -> x0, waiting for transfers between devices: 59.2 us -> none  [shards(): lax.all_gather(out_grad, 'ch', axis=1, tiled=True)]
    all_to_all x0 -> x1, waiting for transfers between devices: none -> 25.9 us  [swapped_in(): return jnp.concatenate(lax.all_to_all(sent, name, 0, 0), axis=along)]
    all_to_all x0 -> x1, starting transfers between devices: none -> 7.23 us  [swapped_in(): return jnp.concatenate(lax.all_to_all(sent, name, 0, 0), axis=along)]
where the time goes in v1:
time: 442 us; the launch traced here: 437 us
  local copies, waits for them, and re-layouts  145 us (33%)
  waiting for transfers between devices  119 us (27%)
  blocking collectives  72 us (16%)
  other arithmetic  38.5 us (9%)
  starting transfers between devices  28.1 us (6%)
  matrix products  19.1 us (4%)
  between operations  15.1 us (3%)
    reduce_scatter x1, waiting for transfers between devices, shards(): lax.psum_scatter(partial_proj, 'ch', scatter_dimension=1, tiled=True)  80.3 us
    pad x20, local copies, waits for them, and re-layouts, prepare(): lax.associative_scan(combine, (block_final_states, factor), axis=1)  42.8 us
    slice x34, local copies, waits for them, and re-layouts, prepare(): lax.associative_scan(combine, (block_final_states, factor), axis=1)  32.8 us
    all_to_all x1, blocking collectives, long_backward(): lax.all_to_all(final_output, 'ctx', split_axis=1, concat_axis=0, tiled=True)  26.1 us
    all_to_all x1, waiting for transfers between devices, swapped_in(): return jnp.concatenate(lax.all_to_all(sent, name, 0, 0), axis=along)  25.9 us
    all_to_all x1, blocking collectives, long_forward(): lax.all_to_all(final_output, 'ctx', split_axis=1, concat_axis=0, tiled=True)  25.2 us
    rev x1, local copies, waits for them, and re-layouts, long_backward(): jnp.flip(finish(within_block, running, decays, jnp.zeros(decays.shape, jn...  23.9 us
    rev x1, local copies, waits for them, and re-layouts, long_backward(): jnp.flip(sequence.astype(jnp.float32), 1)  21.2 us
  transfers between devices with their start and end apart: 5, of which 4 were waited for; matrix products, arithmetic and copies ran while one was open for 3% of the time, Pallas kernels for 0%

profile of v1, /device:TPU:32, one launch (start us, length us, event | category | flops | bytes accessed | tf_op | source)
XLA Modules:
  0.0 437.1 jit_solution(2685100510612163613)
XLA Ops:
  8.1 1.9 collective-permute-start
  11.0 1.6 stack.22
  12.6 7.2 %all-to-all-start.2 = ((bf16[16,256,256]{1,2,0:T(8,128)(2,1)}), bf16[16,256,256]{1,2,0:T(8,128)(2,1)}, u32[]{:S(2)}, u32[]{:S(2)}) async-start(bf16[16,256,256]{1,2,0:T(8,128)(2,1)} %stack.22), calls=%async_computation.3 | async-start | bytes 4194304 | tf_op jit(solution)/shard_map/all_to_all | solution.py:13
  24.2 25.9 %all-to-all-done.2 = bf16[16,256,256]{1,2,0:T(8,128)(2,1)} async-done(((bf16[16,256,256]{1,2,0:T(8,128)(2,1)}), bf16[16,256,256]{1,2,0:T(8,128)(2,1)}, u32[]{:S(2)}, u32[]{:S(2)}) %all-to-all-start.2) | async-done | bytes 2097184 | tf_op jit(solution)/shard_map/all_to_all | solution.py:13
  50.1 2.3 fusion.74
  54.0 16.2 %all-to-all-start.3 = ((bf16[32,8,256]{2,1,0:T(8,128)(2,1)}), bf16[32,8,256]{2,1,0:T(8,128)(2,1)S(1)}, u32[]{:S(2)}, u32[]{:S(2)}) async-start(bf16[32,8,256]{2,1,0:T(8,128)(2,1)} %bitcast.23), calls=%async_computation.4 | async-start | bytes 262144 | tf_op jit(solution)/shard_map/all_to_all | solution.py:93
  70.6 3.4 fusion.73
  74.0 11.8 %all-to-all-done.3 = bf16[32,8,256]{2,1,0:T(8,128)(2,1)S(1)} async-done(((bf16[32,8,256]{2,1,0:T(8,128)(2,1)}), bf16[32,8,256]{2,1,0:T(8,128)(2,1)S(1)}, u32[]{:S(2)}, u32[]{:S(2)}) %all-to-all-start.3) | async-done | bytes 131104 | tf_op jit(solution)/shard_map/all_to_all | solution.py:93
  85.9 21.2 %rev.7 = f32[8,8192]{1,0:T(8,128)} reverse(f32[8,8192]{1,0:T(8,128)S(1)} %bitcast.140), dimensions={1} | reverse | bytes 524288 | tf_op jit(solution)/shard_map/jit(_flip)/rev | solution.py:94
  109.2 1.8 slice.453
  112.1 1.8 slice.423
  122.3 1.6 multiply_add_fusion.3
  123.9 1.6 slice.447
  125.5 1.7 slice.433
  127.2 1.6 slice.432
  128.8 1.6 multiply_add_fusion.2
  130.4 1.6 slice.445
  132.0 1.6 slice.436
  133.6 1.6 slice.435
  137.5 2.7 fusion.17
  146.7 3.2 pad.107
  152.3 3.2 pad.109
  162.4 1.6 pad.161
  164.0 1.6 pad.217
  165.6 2.1 convolution_add_fusion
  169.8 23.9 %rev.8 = f32[8,8192]{1,0:T(8,128)S(1)} reverse(f32[8,8192]{1,0:T(8,128)} %reshape.79), dimensions={1} | reverse | bytes 524288 | tf_op jit(solution)/shard_map/jit(_flip)/rev | solution.py:95
  193.7 26.1 %all_to_all.72 = f32[8,32,256]{2,0,1:T(8,128)} all-to-all(f32[8,32,256]{2,0,1:T(8,128)S(1)} %bitcast.141), channel_id=1, replica_groups=mesh['ctx'=32,'ch'=16] {'ctx'}, dimensions={1} | all-to-all | bytes 524288 | tf_op jit(solution)/shard_map/all_to_all | solution.py:98
  222.7 20.7 %all_to_all.73 = bf16[32,8,256]{2,1,0:T(8,128)(2,1)S(1)} all-to-all(bf16[32,8,256]{2,1,0:T(8,128)(2,1)S(1)} %bitcast.150), channel_id=1, replica_groups=mesh['ctx'=32,'ch'=16] {'ctx'}, dimensions={0} | all-to-all | bytes 262144 | tf_op jit(solution)/shard_map/all_to_all | solution.py:84
  247.7 1.8 slice.420
  261.1 1.6 fusion.71
  263.3 3.1 pad.91
  270.3 4.9 %pad.92 = f32[8,8,16]{1,2,0:T(8,128)} pad(f32[8,4,16]{1,2,0:T(8,128)} %pad_maximum_fusion.1, f32[]{:T(128)} %constant.7.clone.1), padding=0_0_0x0_1_1x0_0_0 | pad | bytes 6148 | tf_op jit(solution)/shard_map/pad | solution.py:58
  275.2 4.9 %pad.93 = f32[8,8,16]{1,2,0:T(8,128)} pad(f32[8,4,16]{1,2,0:T(8,128)} %add.260, f32[]{:T(128)} %constant.7.clone.1), padding=0_0_0x1_0_1x0_0_0 | pad | bytes 6148 | tf_op jit(solution)/shard_map/pad | solution.py:58
  280.1 1.5 add.262
  283.3 3.2 pad.94
  286.6 5.0 %pad.95 = f32[8,16,16]{1,2,0:T(8,128)} pad(f32[8,8,16]{1,2,0:T(8,128)} %add.262, f32[]{:T(128)} %constant.7.clone.1), padding=0_0_0x1_0_1x0_0_0 | pad | bytes 12292 | tf_op jit(solution)/shard_map/pad | solution.py:58
  291.5 1.5 add.264
  294.8 3.3 pad.97
  300.8 3.5 pad.99
  305.3 1.6 pad.159
  306.9 1.6 pad.216
  308.6 2.1 convolution_add_fusion.1
  313.8 25.2 %all_to_all.74 = f32[8,32,256]{2,0,1:T(8,128)S(1)} all-to-all(f32[8,32,256]{2,0,1:T(8,128)S(1)} %copy.87), channel_id=1, replica_groups=mesh['ctx'=32,'ch'=16] {'ctx'}, dimensions={1} | all-to-all | bytes 524288 | tf_op jit(solution)/shard_map/all_to_all | solution.py:89
  339.2 2.7 fusion.24
  342.9 2.5 collective-permute-start.1
  345.5 1.4 collective-permute-done.1
  348.4 80.3 %reduce-scatter.2.cloned.1.call-done = f32[256,256]{1,0:T(8,128)} async-done(((f32[256,4096]{1,0:T(8,128)}), f32[256,256]{1,0:T(8,128)}) %reduce-scatter.2.cloned.1.call-update) | async-done | bytes 262160 | tf_op jit(solution)/shard_map/reduce_scatter | solution.py:121
  428.7 1.6 convert_element_type.43
  (202 shorter events, 75.8 us)
Async XLA Ops:
  7.2 42.9 %copy-start = (bf16[256,4096]{1,0:T(8,128)(2,1)S(1)}, bf16[256,4096]{1,0:T(8,128)(2,1)}, u32[]{:S(2)}) copy-start(bf16[256,4096]{1,0:T(8,128)(2,1)} %param.15) | copy-start | bytes 6291460
  8.1 15.3 %collective-permute-start = (bf16[3,6,256]{2,1,0:T(8,128)(2,1)S(1)}, bf16[3,6,256]{2,1,0:T(8,128)(2,1)S(1)}, u32[]{:S(2)}, u32[]{:S(2)}) collective-permute-start(bf16[3,6,256]{2,1,0:T(8,128)(2,1)S(1)} %pad_maximum_fusion.14), channel_id=1, source_target_pairs={{0,16},{16,32},{32,48},{48,64},{64,80},{80,96},{96,112},{112,128},... | collective-permute-start | bytes 27656 | tf_op jit(solution)/shard_map/ppermute | solution.py:19
  12.5 7.3 %copy-start.34 = (f32[256,16]{0,1:T(8,128)S(1)}, f32[256,16]{0,1:T(8,128)}, u32[]{:S(2)}) copy-start(f32[256,16]{0,1:T(8,128)} %param.14) | copy-start | bytes 49156
  12.5 7.3 %copy-start.35 = (f32[256,16]{0,1:T(8,128)S(1)}, f32[256,16]{0,1:T(8,128)}, u32[]{:S(2)}) copy-start(f32[256,16]{0,1:T(8,128)} %param.13) | copy-start | bytes 49156
  12.6 8.1 %copy-start.33 = (f32[7,3,256]{2,0,1:T(8,128)S(1)}, f32[7,3,256]{2,0,1:T(8,128)}, u32[]{:S(2)}) copy-start(f32[7,3,256]{2,0,1:T(8,128)} %param.12) | copy-start | bytes 64516
  12.6 10.9 %copy-start.13 = (bf16[256,256]{1,0:T(8,128)(2,1)S(1)}, bf16[256,256]{1,0:T(8,128)(2,1)}, u32[]{:S(2)}) copy-start(bf16[256,256]{1,0:T(8,128)(2,1)} %param.11) | copy-start | bytes 393220
  12.6 10.9 %copy-start.14 = (bf16[256,256]{1,0:T(8,128)(2,1)S(1)}, bf16[256,256]{1,0:T(8,128)(2,1)}, u32[]{:S(2)}) copy-start(bf16[256,256]{1,0:T(8,128)(2,1)} %param.10) | copy-start | bytes 393220
  12.6 10.8 %copy-start.15 = (bf16[256,256]{1,0:T(8,128)(2,1)S(1)}, bf16[256,256]{1,0:T(8,128)(2,1)}, u32[]{:S(2)}) copy-start(bf16[256,256]{1,0:T(8,128)(2,1)} %param.9) | copy-start | bytes 393220
  12.6 37.5 %all-to-all-start.2 = ((bf16[16,256,256]{1,2,0:T(8,128)(2,1)}), bf16[16,256,256]{1,2,0:T(8,128)(2,1)}, u32[]{:S(2)}, u32[]{:S(2)}) async-start(bf16[16,256,256]{1,2,0:T(8,128)(2,1)} %stack.22), calls=%async_computation.3 | async-start | bytes 4194304 | tf_op jit(solution)/shard_map/all_to_all | solution.py:13
  20.1 88.1 %copy-start.36 = (f32[64]{0:T(128)}, f32[64]{0:T(128)S(1)}, u32[]{:S(2)}) copy-start(f32[64]{0:T(128)S(1)} %iota_subtract_fusion) | copy-start | bytes 772
  20.7 3.5 copy-start.19
  20.7 3.5 copy-start.21
  20.7 3.5 copy-start.23
  20.7 3.5 copy-start.25
  20.8 3.4 copy-start.27
  20.8 3.4 copy-start.29
  21.4 49.0 %copy-start.17 = (f32[8,16]{1,0:T(8,128)}, f32[8,16]{1,0:T(8,128)S(1)}, u32[]{:S(2)}) copy-start(f32[8,16]{1,0:T(8,128)S(1)} %get-tuple-element.34) | copy-start | bytes 1540
  21.9 2.3 copy-start.31
  52.5 0.7 copy-start.1
  54.0 31.9 %all-to-all-start.3 = ((bf16[32,8,256]{2,1,0:T(8,128)(2,1)}), bf16[32,8,256]{2,1,0:T(8,128)(2,1)S(1)}, u32[]{:S(2)}, u32[]{:S(2)}) async-start(bf16[32,8,256]{2,1,0:T(8,128)(2,1)} %bitcast.23), calls=%async_computation.4 | async-start | bytes 262144 | tf_op jit(solution)/shard_map/all_to_all | solution.py:93
  70.1 358.5 %reduce-scatter.2.cloned.1.call-start = ((), (), s32[]{:S(2)}) async-start(), calls=%async_computation.6 | async-start | bytes 4456448 | tf_op jit(solution)/shard_map/reduce_scatter | solution.py:121
  109.2 4.7 %copy-start.8 = (f32[8,128,16]{1,2,0:T(8,128)}, f32[8,128,16]{1,2,0:T(8,128)S(1)}, u32[]{:S(2)}) copy-start(f32[8,128,16]{1,2,0:T(8,128)S(1)} %fusion.42) | copy-start | bytes 196612
  119.4 15.7 %copy-start.4 = (f32[8,32,16]{1,2,0:T(8,128)}, f32[8,32,16]{1,2,0:T(8,128)S(1)}, u32[]{:S(2)}) copy-start(f32[8,32,16]{1,2,0:T(8,128)S(1)} %multiply_add_fusion.4) | copy-start | bytes 49156
  140.3 5.8 %copy-start.7 = (f32[8,8,16]{1,2,0:T(8,128)S(1)}, f32[8,8,16]{1,2,0:T(8,128)}, u32[]{:S(2)}) copy-start(f32[8,8,16]{1,2,0:T(8,128)} %multiply_add_fusion.2) | copy-start | bytes 12292
  140.3 11.2 %copy-start.6 = (f32[8,16,16]{1,2,0:T(8,128)S(1)}, f32[8,16,16]{1,2,0:T(8,128)}, u32[]{:S(2)}) copy-start(f32[8,16,16]{1,2,0:T(8,128)} %multiply_add_fusion.3) | copy-start | bytes 24580
  140.3 16.2 %copy-start.5 = (f32[8,32,16]{1,2,0:T(8,128)S(1)}, f32[8,32,16]{1,2,0:T(8,128)}, u32[]{:S(2)}) copy-start(f32[8,32,16]{1,2,0:T(8,128)} %copy-done.4) | copy-start | bytes 49156
  144.5 17.8 %copy-start.9 = (f32[8,128,16]{1,2,0:T(8,128)S(1)}, f32[8,128,16]{1,2,0:T(8,128)}, u32[]{:S(2)}) copy-start(f32[8,128,16]{1,2,0:T(8,128)} %copy-done.8) | copy-start | bytes 196612
  146.1 19.5 %copy-start.12 = (f32[8,128,64]{1,2,0:T(8,128)S(1)}, f32[8,128,64]{1,2,0:T(8,128)}, u32[]{:S(2)}) copy-start(f32[8,128,64]{1,2,0:T(8,128)} %fusion.17) | copy-start | bytes 786436
  169.8 75.4 %copy-start.3 = (f32[8,64,64]{2,0,1:T(8,128)S(1)}, f32[8,64,64]{2,0,1:T(8,128)}, u32[]{:S(2)}) copy-start(f32[8,64,64]{2,0,1:T(8,128)} %fusion.73) | copy-start | bytes 393220
  247.7 9.6 %copy-start.16 = (f32[8,16]{1,0:T(8,128)S(1)}, f32[8,16]{1,0:T(8,128)}, u32[]{:S(2)}) copy-start(f32[8,16]{1,0:T(8,128)} %get-tuple-element.30) | copy-start | bytes 1540
  270.3 38.3 %copy-start.11 = (f32[8,128,64]{1,2,0:T(8,128)S(1)}, f32[8,128,64]{1,2,0:T(8,128)}, u32[]{:S(2)}) copy-start(f32[8,128,64]{1,2,0:T(8,128)} %fusion.19) | copy-start | bytes 786436
  293.9 14.7 %copy-start.18 = (f32[8,16]{1,0:T(8,128)S(1)}, f32[8,16]{1,0:T(8,128)}, u32[]{:S(2)}) copy-start(f32[8,16]{1,0:T(8,128)} %copy-done.17) | copy-start | bytes 1540
  341.9 0.9 copy-start.2
  341.9 1.0 copy-start.10
  342.8 4.1 copy-start.20
  342.8 4.1 copy-start.22
  342.8 4.1 copy-start.24
  342.8 4.1 copy-start.26
  342.8 4.1 copy-start.28
  342.8 4.1 copy-start.30
  342.8 4.1 copy-start.32
  342.9 3.9 collective-permute-start.1
Sparse Core Ops, SparseCore 0:
  342.0 86.6 reduce-scatter.1
